TPU v7x, 256 devices: a whole 4x4x8 slice. The times are simulated.
256 devices in a mesh: req: 32 (over z, y), head: 8 (over x, core).
Axes of the slice: x: 4, y: 4, z: 8, core: 2. Of those that a mesh axis runs over, the one named last changes fastest.
Arguments:
- hidden: bfloat16 [512, 2048], P('req'), may hold values from -6 to 6
- deal_order: int32 [512], replicated, may hold values from 0 to 511, each once
- lengths: int32 [512], replicated, may hold values from 1 to 8192, as said below
- page_table: int32 [512, 64], replicated, may hold values from 0 to 2047, as said below
- key_cache: bfloat16 [2048, 128, 8, 128], P('req', None, 'head'), as said below
- value_cache: bfloat16 [2048, 128, 8, 128], P('req', None, 'head'), may hold values from -12 to 12
- attn_gain: float32 [2048], replicated, may hold values from 0.1 to 1.9
- w_query: bfloat16 [2048, 2048], P(None, 'head'), may hold values from -0.125 to 0.125
- w_key: bfloat16 [2048, 1024], P(None, 'head'), may hold values from -0.125 to 0.125
- w_value: bfloat16 [2048, 1024], P(None, 'head'), may hold values from -0.125 to 0.125
- w_gate: bfloat16 [2048, 2048], P(None, 'head'), may hold values from -0.125 to 0.125
- w_out: bfloat16 [2048, 2048], P('head'), may hold values from -1.5 to 1.5
- query_gain: float32 [128], replicated, may hold values from 0.5 to 2
- key_gain: float32 [128], replicated, may hold values from 0.5 to 2
- mlp_gain: float32 [2048], replicated, may hold values from 0.1 to 1.9
- mlp_gate: bfloat16 [2048, 3072], P(None, 'head'), may hold values from -0.125 to 0.125
- mlp_up: bfloat16 [2048, 3072], P(None, 'head'), may hold values from -0.125 to 0.125
- mlp_down: bfloat16 [3072, 2048], P('head'), may hold values from -0.109375 to 0.109375
Outputs:
- output: bfloat16 [512, 2048], P('req')
Inputs may be any that keep to these rules, and one draw needn't show every extreme that they name: `lengths`: one request holds exactly 8192 cached tokens, and all requests together fill at most 2048 pages of 128 tokens. `page_table`: for request r the first ceil(lengths[r] / 128) entries of row r name, in order, the pages that hold its cached tokens; no page is named by two such entries; the other entries are arbitrary page numbers. `key_cache`: cached keys; entries lie within -402 and 402.
All inputs are finite; a program needn't handle non-finite values.
Results may differ from a plain program's by a relative error of at most 0.022.
Values may be sent and summed in bfloat16 or wider, within the bound.
A program may use at most 64 MiB of HBM per device.

v0:
```python
import math
import jax
import jax.numpy as jnp
from jax import lax
from jax.sharding import PartitionSpec as P

EPSILON = 1e-06
ROPE_BASE = 1000000.0
LOW_SCORE = -1e30
LOG_TWO = math.log(2.0)


def rms_inv(values):
    return lax.rsqrt(jnp.mean(values * values, axis=-1, keepdims=True) + EPSILON)


def rotate(values, position):
    half_dim = values.shape[-1] // 2
    exponent = jnp.arange(half_dim, dtype=jnp.float32) * (2.0 / values.shape[-1])
    frequency = ROPE_BASE ** (-exponent)
    angles = position[:, None] * frequency[None, :]
    ones_tail = (1,) * (values.ndim - 2)
    angles = angles.reshape((angles.shape[0],) + ones_tail + (half_dim,))
    cosine = jnp.cos(angles)
    sine_vals = jnp.sin(angles)
    front_half = values[..., :half_dim]
    back_half = values[..., half_dim:]
    return jnp.concatenate(
        [front_half * cosine - back_half * sine_vals, back_half * cosine + front_half * sine_vals],
        axis=-1,
    )


def norm_rotate(values, gain_vec, position):
    return rotate(values * rms_inv(values) * gain_vec, position)


def pick_rows(wanted, shard_rows):
    targets = jnp.arange(shard_rows.shape[0], dtype=jnp.int32)
    selector = (wanted[:, None] == targets[None, :]).astype(jnp.bfloat16)
    return jnp.dot(selector, shard_rows, preferred_element_type=jnp.float32)


def body(
    hidden,
    deal_order,
    lengths,
    page_table,
    key_cache,
    value_cache,
    attn_gain,
    w_query,
    w_key,
    w_value,
    w_gate,
    w_out,
    query_gain,
    key_gain,
    mlp_gain,
    mlp_gate,
    mlp_up,
    mlp_down,
):
    local_rows, model_width = hidden.shape
    req_devices = lax.axis_size("req")
    req_index = lax.axis_index("req")
    all_rows = local_rows * req_devices
    head_width = query_gain.shape[0]
    pool_pages = key_cache.shape[0]
    page_size = key_cache.shape[1]
    local_kv = key_cache.shape[2]
    group_size = w_query.shape[1] // (local_kv * head_width)
    scale_factor = 1.0 / math.sqrt(head_width)
    first_own = req_index * local_rows
    hidden_f = hidden.astype(jnp.float32)
    normed = (hidden_f * rms_inv(hidden_f) * attn_gain).astype(jnp.bfloat16)
    own_requests = lax.dynamic_slice_in_dim(deal_order, first_own, local_rows)
    position = lengths[own_requests].astype(jnp.float32)
    queries = jnp.dot(normed, w_query, preferred_element_type=jnp.float32).reshape(
        local_rows, local_kv, group_size, head_width
    )
    queries = norm_rotate(queries, query_gain, position).astype(jnp.bfloat16)
    new_keys = jnp.dot(normed, w_key, preferred_element_type=jnp.float32).reshape(
        local_rows, local_kv, head_width
    )
    new_keys = norm_rotate(new_keys, key_gain, position).astype(jnp.bfloat16)
    new_values = (
        jnp.dot(normed, w_value, preferred_element_type=jnp.float32)
        .astype(jnp.bfloat16)
        .reshape(local_rows, local_kv, head_width)
    )
    gate_logits = jnp.dot(normed, w_gate, preferred_element_type=jnp.float32)
    all_queries = lax.all_gather(queries, "req", axis=0, tiled=True)
    dealt_lengths = lengths[deal_order]
    dealt_tables = page_table[deal_order]
    page_counts = (dealt_lengths + page_size - 1) // page_size
    slot_ids = jnp.arange(dealt_tables.shape[1], dtype=jnp.int32)
    local_ids = dealt_tables - req_index * pool_pages
    usable = (
        (slot_ids[None, :] < page_counts[:, None]) & (local_ids >= 0) & (local_ids < pool_pages)
    )
    targets = jnp.where(usable, local_ids, pool_pages).reshape(-1)
    request_ids = jnp.broadcast_to(
        jnp.arange(all_rows, dtype=jnp.int32)[:, None], dealt_tables.shape
    ).reshape(-1)
    slot_flat = jnp.broadcast_to(slot_ids[None, :], dealt_tables.shape).reshape(-1)
    owners = jnp.full((pool_pages,), all_rows, jnp.int32).at[targets].set(request_ids, mode="drop")
    owner_slots = jnp.zeros((pool_pages,), jnp.int32).at[targets].set(slot_flat, mode="drop")
    safe_owners = jnp.minimum(owners, all_rows - 1)
    filled = jnp.where(
        owners < all_rows,
        jnp.clip(dealt_lengths[safe_owners] - owner_slots * page_size, 0, page_size),
        0,
    )
    page_queries = all_queries[safe_owners]
    scores = (
        jnp.einsum("pkgd,ptkd->pkgt", page_queries, key_cache, preferred_element_type=jnp.float32)
        * scale_factor
    )
    live_mask = (
        jnp.arange(page_size, dtype=jnp.int32)[None, None, None, :] < filled[:, None, None, None]
    )
    scores = jnp.where(live_mask, scores, LOW_SCORE)
    page_peaks = jnp.max(scores, axis=-1)
    local_peaks = (
        jnp.full((all_rows, local_kv, group_size), LOW_SCORE, jnp.float32)
        .at[owners]
        .max(page_peaks, mode="drop")
    )
    self_scores = (
        jnp.einsum("rkgd,rkd->rkg", queries, new_keys, preferred_element_type=jnp.float32)
        * scale_factor
    )
    own_peaks = jnp.maximum(
        lax.dynamic_slice_in_dim(local_peaks, first_own, local_rows), self_scores
    )
    with_self = lax.dynamic_update_slice_in_dim(local_peaks, own_peaks, first_own, 0)
    global_peaks = lax.pmax(with_self, "req")
    global_shift = LOG_TWO * jnp.ceil(global_peaks / LOG_TWO)
    weights = jnp.where(live_mask, jnp.exp(scores - global_shift[safe_owners][..., None]), 0.0)
    totals = (
        jnp.zeros((all_rows, local_kv, group_size), jnp.float32)
        .at[owners]
        .add(jnp.sum(weights, axis=-1), mode="drop")
    )
    page_numerators = jnp.einsum(
        "pkgt,ptkd->pkgd",
        weights.astype(jnp.bfloat16),
        value_cache,
        preferred_element_type=jnp.float32,
    )
    numerators = (
        jnp.zeros((all_rows, local_kv, group_size, head_width), jnp.float32)
        .at[owners]
        .add(page_numerators, mode="drop")
    )
    totals, numerators = (totals, numerators)
    own_totals, own_numerators = (
        lax.psum_scatter(totals, "req", scatter_dimension=0, tiled=True),
        lax.psum_scatter(numerators, "req", scatter_dimension=0, tiled=True),
    )
    own_shift = lax.dynamic_slice_in_dim(global_shift, first_own, local_rows)
    self_weight = jnp.exp(self_scores - own_shift)
    own_totals = own_totals + self_weight
    self_rounded = lax.optimization_barrier(self_weight.astype(jnp.bfloat16)).astype(jnp.float32)
    own_numerators = (
        own_numerators + self_rounded[..., None] * new_values.astype(jnp.float32)[:, :, None, :]
    )
    heads_out = (own_numerators / own_totals[..., None]).reshape(
        local_rows, local_kv * group_size * head_width
    )
    attended = (heads_out * jax.nn.sigmoid(gate_logits)).astype(jnp.bfloat16)
    projected = jnp.dot(attended, w_out, preferred_element_type=jnp.float32)
    attn_total = lax.psum(projected.astype(jnp.bfloat16), "head").astype(jnp.float32)
    mixed_rows = (hidden_f + attn_total).astype(jnp.bfloat16)
    mixed_f = mixed_rows.astype(jnp.float32)
    normed_two = (mixed_f * rms_inv(mixed_f) * mlp_gain).astype(jnp.bfloat16)
    gate_part = jnp.dot(normed_two, mlp_gate, preferred_element_type=jnp.float32)
    up_part = jnp.dot(normed_two, mlp_up, preferred_element_type=jnp.float32)
    inner_act = (jax.nn.silu(gate_part) * up_part).astype(jnp.bfloat16)
    down_part = jnp.dot(inner_act, mlp_down, preferred_element_type=jnp.float32)
    inverse_order = (
        jnp.zeros((all_rows,), jnp.int32).at[deal_order].set(jnp.arange(all_rows, dtype=jnp.int32))
    )
    wanted = lax.dynamic_slice_in_dim(inverse_order, first_own, local_rows)
    mlp_total = lax.psum(down_part.astype(jnp.bfloat16), "head").astype(jnp.float32)
    result = (mixed_f + mlp_total).astype(jnp.bfloat16)
    gathered = pick_rows(wanted, lax.all_gather(result, "req", axis=0, tiled=True))
    output = gathered.astype(jnp.bfloat16)
    return output


def solution(mesh):
    return jax.shard_map(
        body,
        mesh=mesh,
        in_specs=(
            P("req", None),
            P(),
            P(),
            P(),
            P("req", None, "head", None),
            P("req", None, "head", None),
            P(),
            P(None, "head"),
            P(None, "head"),
            P(None, "head"),
            P(None, "head"),
            P("head", None),
            P(),
            P(),
            P(),
            P(None, "head"),
            P(None, "head"),
            P("head", None),
        ),
        out_specs=P("req", None),
        check_vma=False,
    )
```

profile of v0, /device:TPU:2, one launch (start us, length us, event | category | flops | bytes accessed | tf_op | source)
XLA Modules:
  0.0 1038.4 jit_solution(14262938876819041306)
XLA Ops:
  6.6 0.8 compare_select_fusion.1
  7.5 0.8 compare_select_fusion.2
  8.3 1.0 fusion.17
  9.3 3.6 gather_fusion
  12.9 0.7 gather_fusion.3
  13.6 0.3 fusion.77
  14.0 0.1 iota_compare_fusion
  14.2 0.1 lt.102
  14.3 0.1 multiply_cosine_fusion.1
  14.7 52.5 %all_gather.6 = bf16[512,1,2,128]{3,2,1,0:T(2,128)(2,1)S(1)} all-gather(bf16[16,1,2,128]{3,2,1,0:T(2,128)(2,1)S(1)} %pad_maximum_fusion), channel_id=1, replica_groups=mesh['req'=32,'head'=8] {'req'}, dimensions={0}, use_global_device_ids=true | all-gather | bytes 270336 | tf_op jit(solution)/shard_map/all_gather | solution.py:93
  67.2 0.1 copy.63
  67.3 1.0 gather_fusion.1
  68.4 0.2 sub.57
  68.9 0.4 compare_select_fusion
  69.3 120.0 %scatter_custom_fusion.2 = s32[64]{0:T(128)S(1)} fusion(s32[32768]{0:T(1024)S(1)} %bitcast.102, s32[32768]{0:T(1024)S(1)} %reshape.511, s32[]{:T(128)} %constant.24.clone.1), kind=kCustom, calls=%fused_computation.126 | custom fusion | bytes 260 | tf_op jit(solution)/shard_map/scatter | solution.py:108
  189.3 120.0 %scatter_custom_fusion.1 = s32[64]{0:T(128)S(1)} fusion(s32[32768]{0:T(1024)S(1)} %bitcast.103, s32[32768]{0:T(1024)S(1)} %reshape.503, s32[]{:T(128)} %constant.25.clone.1), kind=kCustom, calls=%fused_computation.128 | custom fusion | bytes 260 | tf_op jit(solution)/shard_map/scatter | solution.py:107
  309.4 0.8 gather_fusion.2
  310.2 0.6 gather_fusion.4
  310.9 1.3 fusion.80
  312.2 0.9 scatter_custom_fusion.3
  313.2 0.4 multiply_reduce_fusion.1
  313.7 0.1 fusion.56
  313.9 0.2 fusion.53
  314.2 0.1 dynamic_update_slice.3
  314.4 72.4 %pmax.7 = f32[512,1,2]{0,2,1:T(2,128)S(1)} all-reduce(f32[512,1,2]{0,2,1:T(2,128)S(1)} %dynamic_update_slice.3), channel_id=1, replica_groups=mesh['req'=32,'head'=8] {'req'}, use_global_device_ids=true, to_apply=%region_8.9 | all-reduce | flops 1024 | bytes 8192 | tf_op jit(solution)/shard_map/pmax | solution.py:138
  386.7 0.1 copy.68
  386.9 0.6 gather_fusion.5
  387.5 0.2 fusion.70
  387.7 1.5 scatter_custom_fusion.5
  389.3 2.3 fusion
  391.6 0.1 broadcast.362
  391.8 2.8 scatter_fusion
  394.6 0.8 copy.88
  395.5 0.2 fusion.16
  395.7 203.3 %reduce-scatter.10.cloned.1.call-done = f32[16,2]{1,0:T(8,128)} async-done(((f32[512,2]{1,0:T(8,128)}), f32[16,2]{1,0:T(8,128)}) %reduce-scatter.10.cloned.1.call-update) | async-done | bytes 144
  599.0 0.8 copy.77
  600.0 214.6 %reduce-scatter.8.cloned.1.call-done = f32[16,256]{1,0:T(8,128)} async-done(((f32[512,256]{1,0:T(8,128)}), f32[16,256]{1,0:T(8,128)}) %reduce-scatter.8.cloned.1.call-update) | async-done | bytes 16400
  814.7 0.7 reshape.564
  815.5 3.0 convolution_convert_fusion.2
  818.5 60.0 %all-reduce.3.cloned.1.call-done = bf16[16,2048]{1,0:T(8,128)(2,1)} async-done(((bf16[16,2048]{1,0:T(8,128)(2,1)}), bf16[16,2048]{1,0:T(8,128)(2,1)}) %all-reduce.3.cloned.1.call-update) | async-done | bytes 65552 | tf_op jit(solution)/shard_map/psum | solution.py:174
  878.5 1.0 fusion.21
  879.5 1.8 fusion.41
  881.3 3.3 convolution_convert_fusion.1
  884.7 62.9 %all-reduce.5.cloned.1.call-done = bf16[16,2048]{1,0:T(8,128)(2,1)} async-done(((bf16[16,2048]{1,0:T(8,128)(2,1)}), bf16[16,2048]{1,0:T(8,128)(2,1)}) %all-reduce.5.cloned.1.call-update) | async-done | bytes 65552 | tf_op jit(solution)/shard_map/psum | solution.py:186
  947.6 1.5 fusion.24
  949.1 2.4 scatter_custom_fusion
  951.6 77.6 %all-gather.2.cloned.1.call-done = bf16[512,2048]{1,0:T(8,128)(2,1)} async-done(((bf16[16,2048]{1,0:T(8,128)(2,1)}), bf16[512,2048]{1,0:T(8,128)(2,1)}) %all-gather.2.cloned.1.call-update) | async-done | bytes 2097168 | tf_op jit(solution)/shard_map/all_gather | solution.py:188
  1029.2 2.6 convolution_convert_fusion
  (70 shorter events, 2.0 us)
Async XLA Ops:
  6.5 304.4 %copy-start = (bf16[64,128,1,128]{3,1,2,0:T(8,128)(2,1)S(1)}, bf16[64,128,1,128]{3,1,2,0:T(8,128)(2,1)}, u32[]{:S(2)}) copy-start(bf16[64,128,1,128]{3,1,2,0:T(8,128)(2,1)} %param.22) | copy-start | bytes 6291460
  6.5 7.1 copy-start.2
  6.5 6.4 copy-start.1
  6.5 7.1 copy-start.6
  6.5 7.1 copy-start.3
  6.5 592.5 %reduce-scatter.10.cloned.1.call-start = ((), (), s32[]{:S(2)}) async-start(), calls=%async_computation.6 | async-start | bytes 270336
  9.2 5.2 copy-start.10
  12.9 54.3 %copy-start.7 = (s32[512,64]{0,1:T(8,128)S(1)}, s32[512,64]{0,1:T(8,128)}, u32[]{:S(2)}) copy-start(s32[512,64]{0,1:T(8,128)} %param.21) | copy-start | bytes 393220
  309.3 3.9 copy-start.4
  310.9 2.7 copy-start.9
  389.3 425.4 %reduce-scatter.8.cloned.1.call-start = ((), (), s32[]{:S(2)}) async-start(), calls=%async_computation.5 | async-start | bytes 540672
  391.6 3.9 copy-start.5
  395.4 484.1 %copy-start.8 = (f32[2048]{0:T(1024)S(1)}, f32[2048]{0:T(1024)}, u32[]{:S(2)}) copy-start(f32[2048]{0:T(1024)} %param.32) | copy-start | bytes 24580
  395.4 483.1 %all-reduce.3.cloned.1.call-start = ((), (), s32[]{:S(2)}) async-start(), calls=%async_computation.2 | async-start | bytes 131072 | tf_op jit(solution)/shard_map/psum | solution.py:174
  818.5 129.1 %all-reduce.5.cloned.1.call-start = ((), (), s32[]{:S(2)}) async-start(), calls=%async_computation.3 | async-start | bytes 131072 | tf_op jit(solution)/shard_map/psum | solution.py:186
  884.6 144.6 %all-gather.2.cloned.1.call-start = ((), (), s32[]{:S(2)}) async-start(), calls=%async_computation.4 | async-start | bytes 2162688 | tf_op jit(solution)/shard_map/all_gather | solution.py:188
Sparse Core Ops, SparseCore 0:
  389.4 209.5 reduce-scatter.9
  603.3 211.3 reduce-scatter.7
  818.6 59.8 all-reduce.2
  884.7 62.8 all-reduce.4
  950.0 79.1 all-gather.1
where the time goes:
time: 1040 us
  waiting for transfers between devices  619 us (60%)
  local copies, waits for them, and re-layouts  254 us (24%)
  blocking collectives  125 us (12%)
  matrix products  15.3 us (1%)
  between operations  13.5 us (1%)
  other arithmetic  12.2 us (1%)
    unnamed x7, waiting for transfers between devices  418 us
    scatter x1, local copies, waits for them, and re-layouts, body(): jnp.zeros((pool_pages,), jnp.int32).at[targets].set(slot_flat, mode='drop')  120 us
    scatter x1, local copies, waits for them, and re-layouts, body(): jnp.full((pool_pages,), all_rows, jnp.int32).at[targets]  120 us
    all_gather x1, waiting for transfers between devices, body(): lax.all_gather(result, 'req', axis=0, tiled=True)  77.6 us
    pmax x1, blocking collectives, body(): global_peaks = lax.pmax(with_self, 'req')  72.4 us
    psum x1, waiting for transfers between devices, body(): lax.psum(down_part.astype(jnp.bfloat16), 'head').astype(jnp.float32)  62.9 us
    psum x1, waiting for transfers between devices, body(): lax.psum(projected.astype(jnp.bfloat16), 'head').astype(jnp.float32)  60 us
    all_gather x1, blocking collectives, body(): all_queries = lax.all_gather(queries, 'req', axis=0, tiled=True)  52.5 us
  transfers between devices with their start and end apart: 5, of which 5 were waited for; matrix products, arithmetic and copies ran while one was open for 1% of the time, Pallas kernels for 0%

commit v1 on v0

--- a/solution.py
+++ b/solution.py
@@ -90,7 +90,9 @@
         .reshape(local_rows, local_kv, head_width)
     )
     gate_logits = jnp.dot(normed, w_gate, preferred_element_type=jnp.float32)
-    all_queries = lax.all_gather(queries, "req", axis=0, tiled=True)
+    all_queries = jnp.concatenate(
+        lax.all_to_all(jnp.stack([queries] * lax.axis_size("req")), "req", 0, 0), axis=0
+    )
     dealt_lengths = lengths[deal_order]
     dealt_tables = page_table[deal_order]
     page_counts = (dealt_lengths + page_size - 1) // page_size

time: 1040 us -> 1000 us (0.962)
  blocking collectives: 125 us -> 74.9 us
  starting transfers between devices: 0.21 us -> 11.8 us
    all_gather x1 -> x0, blocking collectives: 52.5 us -> none  [body(): all_queries = lax.all_gather(queries, 'req', axis=0, tiled=True)]
    all_to_all x0 -> x1, starting transfers between devices: none -> 11.6 us  [body(): lax.all_to_all(jnp.stack([queries] * lax.axis_size('req')), 'req', 0, 0)]
  transfers between devices with their start and end apart: 5 -> 6, of which waited for: 5 -> 5; matrix products, arithmetic and copies ran while one was open for 1% -> 26% of each run, Pallas kernels for 0% -> 0%
where the time goes in v1:
time: 1000 us
  waiting for transfers between devices  618 us (62%)
  local copies, waits for them, and re-layouts  255 us (26%)
  blocking collectives  74.9 us (7%)
  matrix products  16.5 us (2%)
  between operations  13.6 us (1%)
  starting transfers between devices  11.8 us (1%)
  other arithmetic  11.5 us (1%)
    unnamed x7, waiting for transfers between devices  417 us
    scatter x1, local copies, waits for them, and re-layouts, body(): jnp.zeros((pool_pages,), jnp.int32).at[targets].set(slot_flat, mode='drop')  120 us
    scatter x1, local copies, waits for them, and re-layouts, body(): jnp.full((pool_pages,), all_rows, jnp.int32).at[targets]  120 us
    all_gather x1, waiting for transfers between devices, body(): lax.all_gather(result, 'req', axis=0, tiled=True)  77.6 us
    pmax x1, blocking collectives, body(): global_peaks = lax.pmax(with_self, 'req')  74.9 us
    psum x1, waiting for transfers between devices, body(): lax.psum(down_part.astype(jnp.bfloat16), 'head').astype(jnp.float32)  62.9 us
    psum x1, waiting for transfers between devices, body(): lax.psum(projected.astype(jnp.bfloat16), 'head').astype(jnp.float32)  60 us
  transfers between devices with their start and end apart: 6, of which 5 were waited for; matrix products, arithmetic and copies ran while one was open for 26% of the time, Pallas kernels for 0%

profile of v1, /device:TPU:2, one launch (start us, length us, event | category | flops | bytes accessed | tf_op | source)
XLA Modules:
  0.0 1001.5 jit_solution(5545379389266184666)
XLA Ops:
  6.6 1.1 fusion.17
  7.7 0.8 compare_select_fusion.2
  8.5 1.3 gather_fusion.3
  9.8 1.6 fusion.78
  11.5 0.1 multiply_cosine_fusion.1
  11.9 0.8 stack.2
  12.8 11.6 %all-to-all-start = ((bf16[32,16,1,2,128]{4,3,2,1,0:T(2,128)(2,1)}), bf16[32,16,1,2,128]{4,3,2,1,0:T(2,128)(2,1)S(1)}, u32[]{:S(2)}, u32[]{:S(2)}) async-start(bf16[32,16,1,2,128]{4,3,2,1,0:T(2,128)(2,1)} %stack.2), calls=%async_computation | async-start | bytes 524288 | tf_op jit(solution)/shard_map/all_to_all | solution.py:94
  24.5 3.5 gather_fusion
  28.0 0.3 multiply_reduce_fusion.1
  28.5 0.1 fusion.58
  28.7 0.1 fusion.55
  28.9 0.2 iota_compare_fusion
  29.1 0.1 lt.102
  29.2 0.1 copy.57
  29.4 1.0 gather_fusion.1
  30.4 0.2 sub.57
  30.9 0.4 compare_select_fusion
  31.3 120.0 %scatter_custom_fusion.2 = s32[64]{0:T(128)S(1)} fusion(s32[32768]{0:T(1024)S(1)} %bitcast.102, s32[32768]{0:T(1024)S(1)} %reshape.515, s32[]{:T(128)} %constant.24.clone.1), kind=kCustom, calls=%fused_computation.127 | custom fusion | bytes 260 | tf_op jit(solution)/shard_map/scatter | solution.py:110
  151.3 120.0 %scatter_custom_fusion.1 = s32[64]{0:T(128)S(1)} fusion(s32[32768]{0:T(1024)S(1)} %bitcast.103, s32[32768]{0:T(1024)S(1)} %reshape.507, s32[]{:T(128)} %constant.25.clone.1), kind=kCustom, calls=%fused_computation.129 | custom fusion | bytes 260 | tf_op jit(solution)/shard_map/scatter | solution.py:109
  271.4 0.8 gather_fusion.2
  272.3 0.6 gather_fusion.4
  272.9 1.3 fusion.81
  274.2 0.9 scatter_custom_fusion.3
  275.3 0.1 dynamic_update_slice.3
  275.4 74.9 %pmax.7 = f32[512,1,2]{0,2,1:T(2,128)S(1)} all-reduce(f32[512,1,2]{0,2,1:T(2,128)S(1)} %dynamic_update_slice.3), channel_id=1, replica_groups=mesh['req'=32,'head'=8] {'req'}, use_global_device_ids=true, to_apply=%region_8.9 | all-reduce | flops 1024 | bytes 8192 | tf_op jit(solution)/shard_map/pmax | solution.py:140
  350.3 0.1 copy.60
  350.5 0.6 gather_fusion.5
  351.1 0.2 fusion.71
  351.3 1.5 scatter_custom_fusion.5
  352.9 2.3 fusion
  355.2 0.1 broadcast.364
  355.3 2.8 scatter_fusion
  358.2 0.8 copy.80
  359.1 0.2 fusion.16
  359.3 202.8 %reduce-scatter.10.cloned.1.call-done = f32[16,2]{1,0:T(8,128)} async-done(((f32[512,2]{1,0:T(8,128)}), f32[16,2]{1,0:T(8,128)}) %reduce-scatter.10.cloned.1.call-update) | async-done | bytes 144
  562.2 0.8 copy.69
  563.2 214.5 %reduce-scatter.8.cloned.1.call-done = f32[16,256]{1,0:T(8,128)} async-done(((f32[512,256]{1,0:T(8,128)}), f32[16,256]{1,0:T(8,128)}) %reduce-scatter.8.cloned.1.call-update) | async-done | bytes 16400
  777.7 0.7 reshape.569
  778.6 3.0 convolution_convert_fusion.2
  781.6 60.0 %all-reduce.3.cloned.1.call-done = bf16[16,2048]{1,0:T(8,128)(2,1)} async-done(((bf16[16,2048]{1,0:T(8,128)(2,1)}), bf16[16,2048]{1,0:T(8,128)(2,1)}) %all-reduce.3.cloned.1.call-update) | async-done | bytes 65552 | tf_op jit(solution)/shard_map/psum | solution.py:176
  841.6 1.0 fusion.21
  842.6 1.8 fusion.41
  844.4 3.3 convolution_convert_fusion.1
  847.8 62.9 %all-reduce.5.cloned.1.call-done = bf16[16,2048]{1,0:T(8,128)(2,1)} async-done(((bf16[16,2048]{1,0:T(8,128)(2,1)}), bf16[16,2048]{1,0:T(8,128)(2,1)}) %all-reduce.5.cloned.1.call-update) | async-done | bytes 65552 | tf_op jit(solution)/shard_map/psum | solution.py:188
  910.7 1.5 fusion.24
  912.2 2.4 scatter_custom_fusion
  914.7 77.6 %all-gather.2.cloned.1.call-done = bf16[512,2048]{1,0:T(8,128)(2,1)} async-done(((bf16[16,2048]{1,0:T(8,128)(2,1)}), bf16[512,2048]{1,0:T(8,128)(2,1)}) %all-gather.2.cloned.1.call-update) | async-done | bytes 2097168 | tf_op jit(solution)/shard_map/all_gather | solution.py:190
  992.4 2.6 convolution_convert_fusion
  (72 shorter events, 2.0 us)
Async XLA Ops:
  6.5 266.4 %copy-start = (bf16[64,128,1,128]{3,1,2,0:T(8,128)(2,1)S(1)}, bf16[64,128,1,128]{3,1,2,0:T(8,128)(2,1)}, u32[]{:S(2)}) copy-start(bf16[64,128,1,128]{3,1,2,0:T(8,128)(2,1)} %param.22) | copy-start | bytes 6291460
  6.5 17.9 %copy-start.8 = (s32[512]{0:T(512)S(1)}, s32[512]{0:T(512)}, u32[]{:S(2)}) copy-start(s32[512]{0:T(512)} %param.19) | copy-start | bytes 6148
  6.5 17.9 %copy-start.1 = (s32[512]{0:T(512)S(1)}, s32[512]{0:T(512)}, u32[]{:S(2)}) copy-start(s32[512]{0:T(512)} %param.20) | copy-start | bytes 6148
  6.5 5.1 copy-start.10
  11.4 16.6 %copy-start.2 = (bf16[16,2048]{1,0:T(8,128)(2,1)S(1)}, bf16[16,2048]{1,0:T(8,128)(2,1)}, u32[]{:S(2)}) copy-start(bf16[16,2048]{1,0:T(8,128)(2,1)} %param.18) | copy-start | bytes 196612
  11.4 16.6 %copy-start.3 = (bf16[2048,128]{1,0:T(8,128)(2,1)S(1)}, bf16[2048,128]{1,0:T(8,128)(2,1)}, u32[]{:S(2)}) copy-start(bf16[2048,128]{1,0:T(8,128)(2,1)} %param.26) | copy-start | bytes 1572868
  11.4 16.6 %copy-start.5 = (f32[2048]{0:T(1024)S(1)}, f32[2048]{0:T(1024)}, u32[]{:S(2)}) copy-start(f32[2048]{0:T(1024)} %param.24) | copy-start | bytes 24580
  12.8 15.6 %copy-start.9 = (f32[128]{0:T(128)S(1)}, f32[128]{0:T(128)}, u32[]{:S(2)}) copy-start(f32[128]{0:T(128)} %param.31) | copy-start | bytes 1540
  12.8 259.5 %all-to-all-start = ((bf16[32,16,1,2,128]{4,3,2,1,0:T(2,128)(2,1)}), bf16[32,16,1,2,128]{4,3,2,1,0:T(2,128)(2,1)S(1)}, u32[]{:S(2)}, u32[]{:S(2)}) async-start(bf16[32,16,1,2,128]{4,3,2,1,0:T(2,128)(2,1)} %stack.2), calls=%async_computation | async-start | bytes 524288 | tf_op jit(solution)/shard_map/all_to_all | solution.py:94
  24.4 4.8 copy-start.6
  24.4 537.8 %reduce-scatter.10.cloned.1.call-start = ((), (), s32[]{:S(2)}) async-start(), calls=%async_computation.7 | async-start | bytes 270336
  352.8 424.9 %reduce-scatter.8.cloned.1.call-start = ((), (), s32[]{:S(2)}) async-start(), calls=%async_computation.6 | async-start | bytes 540672
  355.2 3.9 copy-start.4
  359.0 483.6 %copy-start.7 = (f32[2048]{0:T(1024)S(1)}, f32[2048]{0:T(1024)}, u32[]{:S(2)}) copy-start(f32[2048]{0:T(1024)} %param.32) | copy-start | bytes 24580
  359.0 482.6 %all-reduce.3.cloned.1.call-start = ((), (), s32[]{:S(2)}) async-start(), calls=%async_computation.3 | async-start | bytes 131072 | tf_op jit(solution)/shard_map/psum | solution.py:176
  781.6 129.1 %all-reduce.5.cloned.1.call-start = ((), (), s32[]{:S(2)}) async-start(), calls=%async_computation.4 | async-start | bytes 131072 | tf_op jit(solution)/shard_map/psum | solution.py:188
  847.7 144.6 %all-gather.2.cloned.1.call-start = ((), (), s32[]{:S(2)}) async-start(), calls=%async_computation.5 | async-start | bytes 2162688 | tf_op jit(solution)/shard_map/all_gather | solution.py:190
Sparse Core Ops, SparseCore 0:
  353.0 209.1 reduce-scatter.9
  566.4 211.2 reduce-scatter.7
  781.7 59.9 all-reduce.2
  847.8 62.8 all-reduce.4
  913.1 79.1 all-gather.1
